TPU v7x, 256 devices: a whole 4x4x8 slice. The times are simulated.
256 devices in a mesh: gx: 64 (over z, x, core), gy: 4 (over y).
Axes of the slice: x: 4, y: 4, z: 8, core: 2. Of those that a mesh axis runs over, the one named last changes fastest.
Arguments:
- adjoint_block: float32 [4, 3, 64, 256, 512], P(None, None, None, 'gx', 'gy'), may hold values from -18 to 18
- base_flow: float32 [2, 3, 64, 256, 512], P(None, None, None, 'gx', 'gy'), may hold values from -4 to 4
- direct_modes: float32 [8, 3, 64, 256, 512], P(None, None, None, 'gx', 'gy'), may hold values from -0.0012207031 to 0.0012207031
- dual_modes: float32 [8, 3, 64, 256, 512], P(None, None, None, 'gx', 'gy'), may hold values from -0.6 to 0.6
Outputs:
- next_block: float32 [4, 3, 64, 256, 512], P(None, None, None, 'gx', 'gy')
- growth: float32 [4, 4], replicated
All inputs are finite; a program needn't handle non-finite values.
Results may differ from a plain program's by a relative error of at most 0.0001.
Values sent between devices are 32-bit elements; how exact they have to be, the bound alone decides.
A program may use at most 128 MiB of HBM per device.

v0:
```python
import math
import jax
import jax.numpy as jnp
from jax import lax
from jax.sharding import PartitionSpec as P

step_size = 0.1
viscosity = 0.2


def padded_2(shard, sides, width):
    for axis, dim in sides:
        count, length = (lax.axis_size(axis), shard.shape[dim])
        up = [(i, (i + 1) % count) for i in range(count - 1)]
        down = [(j, i) for i, j in up]
        last = lax.slice_in_dim(shard, length - width, length, axis=dim)
        leading = lax.slice_in_dim(shard, 0, width, axis=dim)
        before = lax.ppermute(last, axis, up)
        after = lax.ppermute(leading, axis, down)
        shard = jnp.concatenate([before, shard, after], axis=dim)
    return shard


def central_x(padded):
    return 0.5 * (padded[..., 2:, 1:-1] - padded[..., :-2, 1:-1])


def central_y(padded):
    return 0.5 * (padded[..., 1:-1, 2:] - padded[..., 1:-1, :-2])


def central_z(interior):
    return 0.5 * (jnp.roll(interior, -1, axis=-3) - jnp.roll(interior, 1, axis=-3))


def laplace(padded):
    interior = padded[..., 1:-1, 1:-1]
    beside_all = (
        padded[..., 2:, 1:-1]
        + padded[..., :-2, 1:-1]
        + padded[..., 1:-1, 2:]
        + padded[..., 1:-1, :-2]
    )
    beside_all = beside_all + jnp.roll(interior, -1, axis=-3) + jnp.roll(interior, 1, axis=-3)
    return beside_all - 6.0 * interior


def base_terms(padded_base):
    centre = padded_base[..., 1:-1, 1:-1]
    gradients = jnp.stack([central_x(padded_base), central_y(padded_base), central_z(centre)])
    return (centre, gradients)


def adjoint_step(padded, centre, gradients):
    interior = padded[..., 1:-1, 1:-1]
    advect = (
        centre[0] * central_x(padded)
        + centre[1] * central_y(padded)
        + centre[2] * central_z(interior)
    )
    produce = jnp.sum(interior[:, None] * gradients[None], axis=2)
    return interior + step_size * (advect - produce + viscosity * laplace(padded))


def project(left, right):
    return lax.dot_general(
        left,
        right,
        (((1,), (1,)), ((), ())),
        precision=lax.Precision.HIGHEST,
        preferred_element_type=jnp.float32,
    )


def combine_modes(coefficients, modes):
    return jnp.dot(
        coefficients.T, modes, precision=lax.Precision.HIGHEST, preferred_element_type=jnp.float32
    )


def extend_vectors(field):
    vectors, comps, depth, width_x, width_y = field.shape
    merged = field.reshape(vectors * comps, depth, width_x, width_y)
    padded = padded_2(merged, (("gx", 2), ("gy", 3)), 1)
    return padded.reshape(vectors, comps, depth, width_x + 2, width_y + 2)


def body(adjoint_block, base_flow, direct_modes, dual_modes):
    vectors, comps, depth, width_x, width_y = adjoint_block.shape
    mode_count = direct_modes.shape[0]
    row_count = comps * depth * width_x * width_y
    cell_total = float(
        comps * depth * width_x * lax.axis_size("gx") * width_y * lax.axis_size("gy")
    )
    padded_base = padded_2(
        base_flow.reshape(2 * comps, depth, width_x, width_y), (("gx", 2), ("gy", 3)), 1
    )
    padded_base = padded_base.reshape(2, comps, depth, width_x + 2, width_y + 2)
    direct_flat = direct_modes.reshape(mode_count, row_count)
    dual_flat = dual_modes.reshape(mode_count, row_count)
    padded = extend_vectors(adjoint_block)
    for substep in range(2):
        centre, gradients = base_terms(padded_base[substep])
        advanced = adjoint_step(padded, centre, gradients)
        flattened = advanced.reshape(vectors, row_count)
        partial_terms = project(direct_flat, flattened)
        coefficients = lax.psum(partial_terms, ("gx", "gy"))
        deflated = flattened - combine_modes(coefficients, dual_flat)
        if substep == 0:
            padded = extend_vectors(deflated.reshape(advanced.shape))
    gram_matrix = lax.psum(project(deflated, deflated), ("gx", "gy"))
    cholesky_factor = jnp.linalg.cholesky(gram_matrix)
    solved = jax.scipy.linalg.solve_triangular(cholesky_factor, deflated, lower=True)
    next_block = (math.sqrt(cell_total) * solved).reshape(adjoint_block.shape)
    return (next_block, cholesky_factor)


def solution(mesh):
    placed = (
        P(None, None, None, "gx", "gy"),
        P(None, None, None, "gx", "gy"),
        P(None, None, None, "gx", "gy"),
        P(None, None, None, "gx", "gy"),
    )
    return jax.shard_map(
        body,
        mesh=mesh,
        in_specs=placed,
        out_specs=(P(None, None, None, "gx", "gy"), P()),
        check_vma=False,
    )
```

profile of v0, /device:TPU:1, one launch (start us, length us, event | category | flops | bytes accessed | tf_op | source)
XLA Modules:
  0.0 437.2 jit_solution(15457875989147088941)
XLA Ops:
  0.6 2.9 copy.146
  3.5 2.2 fusion.43
  5.7 5.1 %collective-permute-start.4 = (f32[6,64,1,128]{1,3,2,0:T(8,128)}, f32[6,64,1,128]{1,3,2,0:T(8,128)S(1)}, u32[]{:S(2)}, u32[]{:S(2)}) collective-permute-start(f32[6,64,1,128]{1,3,2,0:T(8,128)} %get-tuple-element.41), channel_id=1, source_target_pairs={{4,0},{8,4},{12,8},{16,12},{20,16},{24,20},{28,24},{32,28},{36,32}... | collective-permute-start | bytes 589832 | tf_op jit(solution)/shard_map/ppermute | solution.py:19
  10.9 1.9 collective-permute-start.5
  13.0 1.2 copy-done.5
  15.2 3.1 collective-permute-start.1
  18.3 2.4 collective-permute-start
  20.7 2.3 slice_bitcast_fusion.5
  23.0 2.1 slice_bitcast_fusion.4
  25.1 1.2 fusion.30
  26.3 1.7 copy.149
  28.0 1.7 copy.148
  29.7 1.7 copy.147
  31.4 5.1 %reshape.186 = f32[8,98304]{1,0:T(8,128)} reshape(f32[8,3,64,4,128]{4,3,2,1,0:T(4,128)} %param.7) | data formatting | bytes 6291456 | tf_op jit(solution)/shard_map/reshape | solution.py:100
  36.5 4.9 %fusion.26 = (f32[1,3,64,4,128]{2,4,3,1,0:T(8,128)}, f32[1,3,64,4,128]{2,4,3,1,0:T(8,128)}) fusion(f32[1,3,1,4,128]{2,4,3,1,0:T(8,128)} %get-tuple-element.35, f32[1,3,63,4,128]{2,4,3,1,0:T(8,128)} %get-tuple-element.39, f32[1,3,63,4,128]{2,4,3,1,0:T(8,128)} %get-tuple-element.36, f32[1,3,1,4,128]{2,4,3,1,0:T(8,128)} %get-tuple-element.32, ...), kind=kLoop, calls=%fused_computation.53 | loop fusion | flops 786432 | bytes 2359296 | tf_op jit(solution)/shard_map/mul | solution.py:33
  42.3 2.6 collective-permute-start.7
  44.8 1.3 collective-permute-start.6
  46.1 2.4 fusion.25
  49.3 1.5 fusion.23
  50.9 1.3 pad_maximum_fusion.2
  52.2 3.1 fusion.40
  55.4 2.4 copy.143
  57.8 1.3 collective-permute-start.3
  59.1 2.4 copy.142
  61.5 4.5 %collective-permute-start.2 = (f32[12,64,6,1]{1,3,2,0:T(1,128)S(1)}, f32[12,64,6,1]{1,3,2,0:T(1,128)S(1)}, u32[]{:S(2)}, u32[]{:S(2)}) collective-permute-start(f32[12,64,6,1]{1,3,2,0:T(1,128)S(1)} %copy.142), channel_id=1, source_target_pairs={{0,1},{1,2},{2,3},{4,5},{5,6},{6,7},{8,9},{9,10},{10,11},{12,13},{... | collective-permute-start | bytes 55304 | tf_op jit(solution)/shard_map/ppermute | solution.py:18
  66.0 3.3 pad_maximum_fusion.3
  69.3 2.8 copy.152
  72.2 2.2 copy.145
  74.4 2.2 copy.144
  76.6 4.9 %pad_maximum_fusion.1 = f32[12,64,6,130]{3,1,2,0:T(8,128)S(1)} fusion(f32[12,64,6,1]{3,1,2,0:T(8,128)} %copy.145, f32[12,64,1,128]{3,1,2,0:T(8,128)} %collective-permute-done.1, f32[12,64,4,128]{3,1,2,0:T(8,128)} %bitcast.87, f32[12,64,1,128]{3,1,2,0:T(8,128)} %collective-permute-done, f32[12,64,6,1]{3,1,2,0:T(8,128)} %copy.144), kind=kLoop, calls=%fused_computation.4 | loop fusion | flops 2396160 | bytes 4792320 | tf_op jit(solution)/shard_map/concatenate | solution.py:20
  84.2 2.1 multiply_add_fusion.1
  86.3 2.2 copy.153
  88.5 8.9 %fusion.6 = f32[8,4]{0,1:T(4,128)S(1)} fusion(f32[8,3,64,4,128]{4,3,2,1,0:T(4,128)S(1)} %copy-done, f32[4,3,64,4,128]{4,2,3,1,0:T(8,128)S(1)} %multiply_add_fusion.1), kind=kOutput, calls=%fused_computation.22 | convolution fusion | flops 37748736 | bytes 4718720 | tf_op jit(solution)/shard_map/dot_general | solution.py:66
  97.4 3.6 reshape.185
  101.1 83.8 %psum.21 = f32[8,4]{0,1:T(4,128)S(1)} all-reduce(f32[8,4]{0,1:T(4,128)S(1)} %fusion.6), channel_id=1, replica_groups=mesh['gx'=64,'gy'=4] {'gx','gy'}, use_global_device_ids=true, to_apply=%region_1.2 | all-reduce | flops 32 | bytes 256 | tf_op jit(solution)/shard_map/psum | solution.py:107
  184.9 6.2 %convolution_subtract_fusion.1 = f32[4,98304]{1,0:T(4,128)} fusion(f32[4,98304]{1,0:T(4,128)} %reshape.185, f32[8,4]{0,1:T(4,128)S(1)} %psum.21, f32[8,98304]{1,0:T(8,128)} %reshape.186), kind=kOutput, calls=%fused_computation.2 | convolution fusion | flops 38141952 | bytes 6291584 | tf_op jit(solution)/shard_map/dot_general | solution.py:76
  191.1 3.9 reshape_reshape.3
  195.0 3.6 fusion.41
  198.7 2.6 collective-permute-start.9
  201.3 3.0 collective-permute-start.8
  205.3 1.7 copy.163
  207.8 3.3 copy.159
  211.1 2.2 copy.160
  213.3 2.2 copy.158
  215.5 1.3 pad_maximum_fusion.19
  216.8 1.3 collective-permute-start.11
  218.1 4.0 collective-permute-start.10
  222.1 1.6 pad_maximum_fusion.4
  223.7 2.8 copy.167
  226.6 4.3 pad_maximum_fusion
  230.8 6.3 %copy.161 = f32[12,64,6,130]{3,1,2,0:T(8,128)} copy(f32[12,64,6,130]{1,3,2,0:T(8,128)} %pad_maximum_fusion) | data formatting | bytes 4792320 | tf_op jit(solution)/shard_map/concatenate | solution.py:20
  237.2 2.4 slice.360
  239.5 3.9 fusion.36
  245.0 2.3 multiply_add_fusion
  247.4 2.2 copy.168
  249.5 8.9 %fusion.11 = f32[8,4]{0,1:T(4,128)S(1)} fusion(f32[8,3,64,4,128]{4,3,2,1,0:T(4,128)S(1)} %copy-done, f32[4,3,64,4,128]{4,2,3,1,0:T(8,128)S(1)} %multiply_add_fusion), kind=kOutput, calls=%fused_computation.23 | convolution fusion | flops 37748736 | bytes 4718720 | tf_op jit(solution)/shard_map/dot_general | solution.py:66
  258.5 3.6 reshape.188
  262.1 75.8 %psum.22 = f32[8,4]{0,1:T(4,128)S(1)} all-reduce(f32[8,4]{0,1:T(4,128)S(1)} %fusion.11), channel_id=1, replica_groups=mesh['gx'=64,'gy'=4] {'gx','gy'}, use_global_device_ids=true, to_apply=%region_3.4 | all-reduce | flops 32 | bytes 256 | tf_op jit(solution)/shard_map/psum | solution.py:107
  337.9 5.1 %convolution_subtract_fusion = f32[4,98304]{1,0:T(4,128)S(1)} fusion(f32[4,98304]{1,0:T(4,128)} %reshape.188, f32[8,4]{0,1:T(4,128)S(1)} %psum.22, f32[8,98304]{1,0:T(8,128)} %reshape.186), kind=kOutput, calls=%fused_computation.1 | convolution fusion | flops 38141952 | bytes 6291584 | tf_op jit(solution)/shard_map/dot_general | solution.py:76
  344.2 6.8 %fusion.44 = f32[4,4]{0,1:T(4,128)S(1)} fusion(f32[4,98304]{1,0:T(4,128)S(1)} %convolution_subtract_fusion), kind=kOutput, calls=%fused_computation.91 | convolution fusion | flops 18874368 | bytes 1572928 | tf_op jit(solution)/shard_map/dot_general | solution.py:66
  351.0 73.8 %psum.23 = f32[4,4]{0,1:T(4,128)S(1)} all-reduce(f32[4,4]{0,1:T(4,128)S(1)} %fusion.44), channel_id=1, replica_groups=mesh['gx'=64,'gy'=4] {'gx','gy'}, use_global_device_ids=true, to_apply=%region_4.5 | all-reduce | flops 16 | bytes 128 | tf_op jit(solution)/shard_map/psum | solution.py:111
  426.0 1.3 select_bitcast_fusion
  427.6 5.5 %convolution_multiply_fusion = f32[4,98304]{1,0:T(4,128)} fusion(f32[4,98304]{1,0:T(4,128)} %copy-done.4, f32[1,4,4]{1,2,0:T(4,128)S(1)} %custom-call.7), kind=kOutput, calls=%fused_computation | convolution fusion | flops 19267584 | bytes 3145792 | tf_op jit(solution)/shard_map/jit(_solve_triangular)/triangular_solve | solution.py:113
  433.1 3.9 reshape.189
  (66 shorter events, 11.7 us)
Async XLA Ops:
  0.6 87.9 %copy-start = (f32[8,3,64,4,128]{4,3,2,1,0:T(4,128)S(1)}, f32[8,3,64,4,128]{4,3,2,1,0:T(4,128)}, u32[]{:S(2)}) copy-start(f32[8,3,64,4,128]{4,3,2,1,0:T(4,128)} %param.6) | copy-start | bytes 9437188
  3.5 9.2 %copy-start.12 = (f32[4,3,64,4,128]{4,3,2,1,0:T(4,128)S(1)}, f32[4,3,64,4,128]{4,3,2,1,0:T(4,128)}, u32[]{:S(2)}) copy-start(f32[4,3,64,4,128]{4,3,2,1,0:T(4,128)} %param.4) | copy-start | bytes 4718596
  5.7 35.7 %collective-permute-start.4 = (f32[6,64,1,128]{1,3,2,0:T(8,128)}, f32[6,64,1,128]{1,3,2,0:T(8,128)S(1)}, u32[]{:S(2)}, u32[]{:S(2)}) collective-permute-start(f32[6,64,1,128]{1,3,2,0:T(8,128)} %get-tuple-element.41), channel_id=1, source_target_pairs={{4,0},{8,4},{12,8},{16,12},{20,16},{24,20},{28,24},{32,28},{36,32}... | collective-permute-start | bytes 589832 | tf_op jit(solution)/shard_map/ppermute | solution.py:19
  10.9 30.6 %collective-permute-start.5 = (f32[6,64,1,128]{1,3,2,0:T(8,128)}, f32[6,64,1,128]{1,3,2,0:T(8,128)}, u32[]{:S(2)}, u32[]{:S(2)}) collective-permute-start(f32[6,64,1,128]{1,3,2,0:T(8,128)} %get-tuple-element.40), channel_id=1, source_target_pairs={{0,4},{4,8},{8,12},{12,16},{16,20},{20,24},{24,28},{28,32},{32,36}... | collective-permute-start | bytes 589832 | tf_op jit(solution)/shard_map/ppermute | solution.py:18
  13.0 1.2 copy-start.5
  13.0 7.7 %copy-start.1 = (f32[2,3,64,4,128]{2,4,3,1,0:T(8,128)S(1)}, f32[2,3,64,4,128]{2,4,3,1,0:T(8,128)}, u32[]{:S(2)}) copy-start(f32[2,3,64,4,128]{2,4,3,1,0:T(8,128)} %copy.146) | copy-start | bytes 2359300
  15.2 35.7 %collective-permute-start.1 = (f32[12,64,1,128]{3,1,2,0:T(8,128)}, f32[12,64,1,128]{3,1,2,0:T(8,128)}, u32[]{:S(2)}, u32[]{:S(2)}) collective-permute-start(f32[12,64,1,128]{3,1,2,0:T(8,128)} %get-tuple-element.31), channel_id=1, source_target_pairs={{4,0},{8,4},{12,8},{16,12},{20,16},{24,20},{28,24},{32,28},{36,32}... | collective-permute-start | bytes 1179656 | tf_op jit(solution)/shard_map/ppermute | solution.py:19
  18.3 32.6 %collective-permute-start = (f32[12,64,1,128]{3,1,2,0:T(8,128)}, f32[12,64,1,128]{3,1,2,0:T(8,128)}, u32[]{:S(2)}, u32[]{:S(2)}) collective-permute-start(f32[12,64,1,128]{3,1,2,0:T(8,128)} %get-tuple-element.30), channel_id=1, source_target_pairs={{0,4},{4,8},{8,12},{12,16},{16,20},{20,24},{24,28},{28,32},{32,36}... | collective-permute-start | bytes 1179656 | tf_op jit(solution)/shard_map/ppermute | solution.py:18
  36.5 4.9 %copy-start.2 = (f32[2,3,64,4,128]{2,4,3,1,0:T(8,128)S(1)}, f32[2,3,64,4,128]{2,4,3,1,0:T(8,128)}, u32[]{:S(2)}) copy-start(f32[2,3,64,4,128]{2,4,3,1,0:T(8,128)} %copy.146) | copy-start | bytes 2359300
  42.3 6.3 %collective-permute-start.7 = (f32[6,64,6,1]{1,3,2,0:T(1,128)S(1)}, f32[6,64,6,1]{1,3,2,0:T(1,128)S(1)}, u32[]{:S(2)}, u32[]{:S(2)}) collective-permute-start(f32[6,64,6,1]{1,3,2,0:T(1,128)S(1)} %get-tuple-element.21), channel_id=1, source_target_pairs={{0,1},{1,2},{2,3},{4,5},{5,6},{6,7},{8,9},{9,10},{10,11},{12,13},{... | collective-permute-start | bytes 27656 | tf_op jit(solution)/shard_map/ppermute | solution.py:18
  44.8 4.5 %collective-permute-start.6 = (f32[6,64,6,1]{1,3,2,0:T(1,128)S(1)}, f32[6,64,6,1]{1,3,2,0:T(1,128)S(1)}, u32[]{:S(2)}, u32[]{:S(2)}) collective-permute-start(f32[6,64,6,1]{1,3,2,0:T(1,128)S(1)} %get-tuple-element.20), channel_id=1, source_target_pairs={{1,0},{2,1},{3,2},{5,4},{6,5},{7,6},{9,8},{10,9},{11,10},{13,12},{... | collective-permute-start | bytes 27656 | tf_op jit(solution)/shard_map/ppermute | solution.py:19
  48.5 2.4 copy-start.6
  57.8 14.4 %collective-permute-start.3 = (f32[12,64,6,1]{1,3,2,0:T(1,128)S(1)}, f32[12,64,6,1]{1,3,2,0:T(1,128)S(1)}, u32[]{:S(2)}, u32[]{:S(2)}) collective-permute-start(f32[12,64,6,1]{1,3,2,0:T(1,128)S(1)} %copy.143), channel_id=1, source_target_pairs={{1,0},{2,1},{3,2},{5,4},{6,5},{7,6},{9,8},{10,9},{11,10},{13,12},{... | collective-permute-start | bytes 55304 | tf_op jit(solution)/shard_map/ppermute | solution.py:19
  61.5 12.9 %collective-permute-start.2 = (f32[12,64,6,1]{1,3,2,0:T(1,128)S(1)}, f32[12,64,6,1]{1,3,2,0:T(1,128)S(1)}, u32[]{:S(2)}, u32[]{:S(2)}) collective-permute-start(f32[12,64,6,1]{1,3,2,0:T(1,128)S(1)} %copy.142), channel_id=1, source_target_pairs={{0,1},{1,2},{2,3},{4,5},{5,6},{6,7},{8,9},{9,10},{10,11},{12,13},{... | collective-permute-start | bytes 55304 | tf_op jit(solution)/shard_map/ppermute | solution.py:18
  81.9 1.3 copy-start.7
  83.2 0.9 copy-start.14
  83.2 1.0 copy-start.15
  83.2 1.0 copy-start.16
  195.0 12.0 %copy-start.13 = (f32[64,4,128]{0,2,1:T(8,128)S(1)}, f32[64,4,128]{0,2,1:T(8,128)}, u32[]{:S(2)}) copy-start(f32[64,4,128]{0,2,1:T(8,128)} %get-tuple-element.22) | copy-start | bytes 393220
  198.7 12.4 %collective-permute-start.9 = (f32[12,64,1,128]{3,1,2,0:T(8,128)}, f32[12,64,1,128]{3,1,2,0:T(8,128)}, u32[]{:S(2)}, u32[]{:S(2)}) collective-permute-start(f32[12,64,1,128]{3,1,2,0:T(8,128)} %bitcast.36), channel_id=1, source_target_pairs={{4,0},{8,4},{12,8},{16,12},{20,16},{24,20},{28,24},{32,28},{36,32}... | collective-permute-start | bytes 1179656 | tf_op jit(solution)/shard_map/ppermute | solution.py:19
  201.3 12.1 %collective-permute-start.8 = (f32[12,64,1,128]{3,1,2,0:T(8,128)}, f32[12,64,1,128]{3,1,2,0:T(8,128)}, u32[]{:S(2)}, u32[]{:S(2)}) collective-permute-start(f32[12,64,1,128]{3,1,2,0:T(8,128)} %bitcast.35), channel_id=1, source_target_pairs={{0,4},{4,8},{8,12},{12,16},{16,20},{20,24},{24,28},{28,32},{32,36}... | collective-permute-start | bytes 1179656 | tf_op jit(solution)/shard_map/ppermute | solution.py:18
  215.5 6.6 %copy-start.9 = (f32[1,3,64,4,128]{2,4,3,1,0:T(8,128)S(1)}, f32[1,3,64,4,128]{2,4,3,1,0:T(8,128)}, u32[]{:S(2)}) copy-start(f32[1,3,64,4,128]{2,4,3,1,0:T(8,128)} %get-tuple-element.15) | copy-start | bytes 1179652
  215.5 6.6 %copy-start.10 = (f32[1,3,64,4,128]{2,4,3,1,0:T(8,128)S(1)}, f32[1,3,64,4,128]{2,4,3,1,0:T(8,128)}, u32[]{:S(2)}) copy-start(f32[1,3,64,4,128]{2,4,3,1,0:T(8,128)} %get-tuple-element.19) | copy-start | bytes 1179652
  215.5 6.6 %copy-start.11 = (f32[1,3,64,4,128]{2,4,3,1,0:T(8,128)S(1)}, f32[1,3,64,4,128]{2,4,3,1,0:T(8,128)}, u32[]{:S(2)}) copy-start(f32[1,3,64,4,128]{2,4,3,1,0:T(8,128)} %get-tuple-element.43) | copy-start | bytes 1179652
  216.8 9.8 %collective-permute-start.11 = (f32[12,64,6,1]{1,3,2,0:T(1,128)S(1)}, f32[12,64,6,1]{1,3,2,0:T(1,128)S(1)}, u32[]{:S(2)}, u32[]{:S(2)}) collective-permute-start(f32[12,64,6,1]{1,3,2,0:T(1,128)S(1)} %get-tuple-element.9), channel_id=1, source_target_pairs={{1,0},{2,1},{3,2},{5,4},{6,5},{7,6},{9,8},{10,9},{11,10},{13,12},{... | collective-permute-start | bytes 55304 | tf_op jit(solution)/shard_map/ppermute | solution.py:19
  218.1 8.5 %collective-permute-start.10 = (f32[12,64,6,1]{1,3,2,0:T(1,128)S(1)}, f32[12,64,6,1]{1,3,2,0:T(1,128)S(1)}, u32[]{:S(2)}, u32[]{:S(2)}) collective-permute-start(f32[12,64,6,1]{1,3,2,0:T(1,128)S(1)} %get-tuple-element.8), channel_id=1, source_target_pairs={{0,1},{1,2},{2,3},{4,5},{5,6},{6,7},{8,9},{9,10},{10,11},{12,13},{... | collective-permute-start | bytes 55304 | tf_op jit(solution)/shard_map/ppermute | solution.py:18
  239.5 4.2 copy-start.3
  239.5 4.5 %copy-start.8 = (f32[3,3,64,4,128]{4,2,3,1,0:T(8,128)S(1)}, f32[3,3,64,4,128]{4,2,3,1,0:T(8,128)}, u32[]{:S(2)}) copy-start(f32[3,3,64,4,128]{4,2,3,1,0:T(8,128)} %copy.167) | copy-start | bytes 3538948
  244.1 0.9 copy-start.17
  244.1 1.0 copy-start.18
  343.0 1.1 copy-start.4
where the time goes:
time: 444 us; the launch traced here: 437 us
  blocking collectives  233 us (52%)
  local copies, waits for them, and re-layouts  91.6 us (21%)
  matrix products  41.5 us (9%)
  other arithmetic  35.5 us (8%)
  starting transfers between devices  33.1 us (7%)
    psum x2, blocking collectives, body(): coefficients = lax.psum(partial_terms, ('gx', 'gy'))  160 us
    psum x1, blocking collectives, body(): gram_matrix = lax.psum(project(deflated, deflated), ('gx', 'gy'))  73.8 us
    dot_general x3, matrix products, project(): lax.dot_general(left, right, (((1,), (1,)), ((), ())), precision=lax.Prec...  24.7 us
    ppermute x6, starting transfers between devices, padded_2(): before = lax.ppermute(last, axis, up)  18.4 us
    ppermute x6, starting transfers between devices, padded_2(): after = lax.ppermute(leading, axis, down)  14.7 us
    slice x5, local copies, waits for them, and re-layouts, padded_2(): last = lax.slice_in_dim(shard, length - width, length, axis=dim)  12.3 us
    dot_general x2, matrix products, combine_modes(): jnp.dot(coefficients.T, modes, precision=lax.Precision.HIGHEST, preferred...  11.3 us
    concatenate x3, other arithmetic, padded_2(): shard = jnp.concatenate([before, shard, after], axis=dim)  10.5 us
  transfers between devices with their start and end apart: 12, of which 1 were waited for; matrix products, arithmetic and copies ran while one was open for 12% of the time, Pallas kernels for 0%

commit v1 on v0

--- a/solution.py
+++ b/solution.py
@@ -108,7 +108,7 @@
         deflated = flattened - combine_modes(coefficients, dual_flat)
         if substep == 0:
             padded = extend_vectors(deflated.reshape(advanced.shape))
-    gram_matrix = lax.psum(project(deflated, deflated), ("gx", "gy"))
+    gram_matrix = lax.psum(lax.psum(project(deflated, deflated), "gy"), "gx")
     cholesky_factor = jnp.linalg.cholesky(gram_matrix)
     solved = jax.scipy.linalg.solve_triangular(cholesky_factor, deflated, lower=True)
     next_block = (math.sqrt(cell_total) * solved).reshape(adjoint_block.shape)

time: 444 us -> 505 us (1.14)
  blocking collectives: 233 us -> 294 us
    psum x1 -> x2, blocking collectives: 73.8 us -> 134 us  [body(): gram_matrix = lax.psum(lax.psum(project(deflated, deflated), 'gy'), 'gx')]
  transfers between devices with their start and end apart: 12 -> 12, of which waited for: 1 -> 1; matrix products, arithmetic and copies ran while one was open for 12% -> 10% of each run, Pallas kernels for 0% -> 0%
where the time goes in v1:
time: 505 us; the launch traced here: 498 us
  blocking collectives  294 us (58%)
  local copies, waits for them, and re-layouts  91.5 us (18%)
  matrix products  41.5 us (8%)
  other arithmetic  35.4 us (7%)
  starting transfers between devices  33.1 us (7%)
    psum x2, blocking collectives, body(): coefficients = lax.psum(partial_terms, ('gx', 'gy'))  160 us
    psum x2, blocking collectives, body(): gram_matrix = lax.psum(lax.psum(project(deflated, deflated), 'gy'), 'gx')  134 us
    dot_general x3, matrix products, project(): lax.dot_general(left, right, (((1,), (1,)), ((), ())), precision=lax.Prec...  24.7 us
    ppermute x6, starting transfers between devices, padded_2(): before = lax.ppermute(last, axis, up)  18.4 us
    ppermute x6, starting transfers between devices, padded_2(): after = lax.ppermute(leading, axis, down)  14.7 us
    slice x5, local copies, waits for them, and re-layouts, padded_2(): last = lax.slice_in_dim(shard, length - width, length, axis=dim)  12.3 us
    dot_general x2, matrix products, combine_modes(): jnp.dot(coefficients.T, modes, precision=lax.Precision.HIGHEST, preferred...  11.3 us
    concatenate x3, other arithmetic, padded_2(): shard = jnp.concatenate([before, shard, after], axis=dim)  10.5 us
  transfers between devices with their start and end apart: 12, of which 1 were waited for; matrix products, arithmetic and copies ran while one was open for 10% of the time, Pallas kernels for 0%

profile of v1, /device:TPU:1, one launch (start us, length us, event | category | flops | bytes accessed | tf_op | source)
XLA Modules:
  0.0 497.6 jit_solution(13332402243412527005)
XLA Ops:
  0.6 2.9 copy.146
  3.5 2.2 fusion.43
  5.7 5.1 %collective-permute-start.4 = (f32[6,64,1,128]{1,3,2,0:T(8,128)}, f32[6,64,1,128]{1,3,2,0:T(8,128)S(1)}, u32[]{:S(2)}, u32[]{:S(2)}) collective-permute-start(f32[6,64,1,128]{1,3,2,0:T(8,128)} %get-tuple-element.41), channel_id=1, source_target_pairs={{4,0},{8,4},{12,8},{16,12},{20,16},{24,20},{28,24},{32,28},{36,32}... | collective-permute-start | bytes 589832 | tf_op jit(solution)/shard_map/ppermute | solution.py:19
  10.9 1.9 collective-permute-start.5
  13.1 1.2 copy-done.5
  15.2 3.1 collective-permute-start.1
  18.3 2.4 collective-permute-start
  20.7 2.2 slice_bitcast_fusion.5
  23.0 2.1 slice_bitcast_fusion.4
  26.2 1.7 copy.149
  27.9 1.7 copy.148
  29.7 1.7 copy.147
  31.4 5.1 %reshape.186 = f32[8,98304]{1,0:T(8,128)} reshape(f32[8,3,64,4,128]{4,3,2,1,0:T(4,128)} %param.7) | data formatting | bytes 6291456 | tf_op jit(solution)/shard_map/reshape | solution.py:100
  36.5 4.9 fusion.26
  42.2 2.6 collective-permute-start.7
  44.8 1.3 collective-permute-start.6
  46.1 2.4 fusion.25
  49.3 1.5 fusion.23
  50.9 1.3 pad_maximum_fusion.2
  52.2 3.1 fusion.40
  55.3 2.4 copy.143
  57.7 1.3 collective-permute-start.3
  59.0 2.4 copy.142
  61.5 4.5 collective-permute-start.2
  66.0 3.3 pad_maximum_fusion.3
  69.3 2.8 copy.152
  72.1 2.2 copy.145
  74.3 2.2 copy.144
  76.5 4.9 pad_maximum_fusion.1
  84.2 2.1 multiply_add_fusion.1
  86.3 2.2 copy.153
  88.4 8.9 %fusion.6 = f32[8,4]{0,1:T(4,128)S(1)} fusion(f32[8,3,64,4,128]{4,3,2,1,0:T(4,128)S(1)} %copy-done, f32[4,3,64,4,128]{4,2,3,1,0:T(8,128)S(1)} %multiply_add_fusion.1), kind=kOutput, calls=%fused_computation.22 | convolution fusion | flops 37748736 | bytes 4718720 | tf_op jit(solution)/shard_map/dot_general | solution.py:66
  97.4 3.6 reshape.185
  101.0 83.8 %psum.28 = f32[8,4]{0,1:T(4,128)S(1)} all-reduce(f32[8,4]{0,1:T(4,128)S(1)} %fusion.6), channel_id=1, replica_groups=mesh['gx'=64,'gy'=4] {'gx','gy'}, use_global_device_ids=true, to_apply=%region_1.2 | all-reduce | flops 32 | bytes 256 | tf_op jit(solution)/shard_map/psum | solution.py:107
  184.8 6.2 %convolution_subtract_fusion.1 = f32[4,98304]{1,0:T(4,128)} fusion(f32[4,98304]{1,0:T(4,128)} %reshape.185, f32[8,4]{0,1:T(4,128)S(1)} %psum.28, f32[8,98304]{1,0:T(8,128)} %reshape.186), kind=kOutput, calls=%fused_computation.2 | convolution fusion | flops 38141952 | bytes 6291584 | tf_op jit(solution)/shard_map/dot_general | solution.py:76
  191.0 3.9 reshape_reshape.3
  194.9 3.6 fusion.41
  198.6 2.6 collective-permute-start.9
  201.1 3.0 collective-permute-start.8
  205.2 1.7 copy.163
  207.7 3.3 copy.159
  211.0 2.2 copy.160
  213.2 2.2 copy.158
  215.3 1.3 pad_maximum_fusion.19
  216.6 1.3 collective-permute-start.11
  217.9 4.0 collective-permute-start.10
  222.0 1.6 pad_maximum_fusion.4
  223.6 2.8 copy.167
  226.4 4.3 pad_maximum_fusion
  230.7 6.3 %copy.161 = f32[12,64,6,130]{3,1,2,0:T(8,128)} copy(f32[12,64,6,130]{1,3,2,0:T(8,128)} %pad_maximum_fusion) | data formatting | bytes 4792320 | tf_op jit(solution)/shard_map/concatenate | solution.py:20
  237.0 2.4 slice.360
  239.4 3.9 fusion.36
  244.9 2.3 multiply_add_fusion
  247.2 2.2 copy.168
  249.4 8.9 %fusion.11 = f32[8,4]{0,1:T(4,128)S(1)} fusion(f32[8,3,64,4,128]{4,3,2,1,0:T(4,128)S(1)} %copy-done, f32[4,3,64,4,128]{4,2,3,1,0:T(8,128)S(1)} %multiply_add_fusion), kind=kOutput, calls=%fused_computation.23 | convolution fusion | flops 37748736 | bytes 4718720 | tf_op jit(solution)/shard_map/dot_general | solution.py:66
  258.3 3.6 reshape.188
  261.9 75.8 %psum.29 = f32[8,4]{0,1:T(4,128)S(1)} all-reduce(f32[8,4]{0,1:T(4,128)S(1)} %fusion.11), channel_id=1, replica_groups=mesh['gx'=64,'gy'=4] {'gx','gy'}, use_global_device_ids=true, to_apply=%region_3.4 | all-reduce | flops 32 | bytes 256 | tf_op jit(solution)/shard_map/psum | solution.py:107
  337.8 5.1 %convolution_subtract_fusion = f32[4,98304]{1,0:T(4,128)S(1)} fusion(f32[4,98304]{1,0:T(4,128)} %reshape.188, f32[8,4]{0,1:T(4,128)S(1)} %psum.29, f32[8,98304]{1,0:T(8,128)} %reshape.186), kind=kOutput, calls=%fused_computation.1 | convolution fusion | flops 38141952 | bytes 6291584 | tf_op jit(solution)/shard_map/dot_general | solution.py:76
  344.0 6.8 %fusion.44 = f32[4,4]{0,1:T(4,128)S(1)} fusion(f32[4,98304]{1,0:T(4,128)S(1)} %convolution_subtract_fusion), kind=kOutput, calls=%fused_computation.91 | convolution fusion | flops 18874368 | bytes 1572928 | tf_op jit(solution)/shard_map/dot_general | solution.py:66
  350.8 8.4 %psum.30 = f32[4,4]{0,1:T(4,128)S(1)} all-reduce(f32[4,4]{0,1:T(4,128)S(1)} %fusion.44), channel_id=1, replica_groups=mesh['gx'=64,'gy'=4] {'gy'}, use_global_device_ids=true, to_apply=%region_4.5 | all-reduce | flops 16 | bytes 128 | tf_op jit(solution)/shard_map/psum | solution.py:111
  359.2 126.1 %psum.31 = f32[4,4]{0,1:T(4,128)S(1)} all-reduce(f32[4,4]{0,1:T(4,128)S(1)} %psum.30), channel_id=1, replica_groups=mesh['gx'=64,'gy'=4] {'gx'}, use_global_device_ids=true, to_apply=%region_5.6 | all-reduce | flops 16 | bytes 128 | tf_op jit(solution)/shard_map/psum | solution.py:111
  486.4 1.2 select_bitcast_fusion
  488.0 5.5 %convolution_multiply_fusion = f32[4,98304]{1,0:T(4,128)} fusion(f32[4,98304]{1,0:T(4,128)} %copy-done.4, f32[1,4,4]{1,2,0:T(4,128)S(1)} %custom-call.7), kind=kOutput, calls=%fused_computation | convolution fusion | flops 19267584 | bytes 3145792 | tf_op jit(solution)/shard_map/jit(_solve_triangular)/triangular_solve | solution.py:113
  493.5 3.9 reshape.189
  (67 shorter events, 12.8 us)
Async XLA Ops:
  0.6 87.8 %copy-start = (f32[8,3,64,4,128]{4,3,2,1,0:T(4,128)S(1)}, f32[8,3,64,4,128]{4,3,2,1,0:T(4,128)}, u32[]{:S(2)}) copy-start(f32[8,3,64,4,128]{4,3,2,1,0:T(4,128)} %param.6) | copy-start | bytes 9437188
  3.5 9.3 %copy-start.12 = (f32[4,3,64,4,128]{4,3,2,1,0:T(4,128)S(1)}, f32[4,3,64,4,128]{4,3,2,1,0:T(4,128)}, u32[]{:S(2)}) copy-start(f32[4,3,64,4,128]{4,3,2,1,0:T(4,128)} %param.4) | copy-start | bytes 4718596
  5.7 35.7 %collective-permute-start.4 = (f32[6,64,1,128]{1,3,2,0:T(8,128)}, f32[6,64,1,128]{1,3,2,0:T(8,128)S(1)}, u32[]{:S(2)}, u32[]{:S(2)}) collective-permute-start(f32[6,64,1,128]{1,3,2,0:T(8,128)} %get-tuple-element.41), channel_id=1, source_target_pairs={{4,0},{8,4},{12,8},{16,12},{20,16},{24,20},{28,24},{32,28},{36,32}... | collective-permute-start | bytes 589832 | tf_op jit(solution)/shard_map/ppermute | solution.py:19
  10.9 30.5 %collective-permute-start.5 = (f32[6,64,1,128]{1,3,2,0:T(8,128)}, f32[6,64,1,128]{1,3,2,0:T(8,128)}, u32[]{:S(2)}, u32[]{:S(2)}) collective-permute-start(f32[6,64,1,128]{1,3,2,0:T(8,128)} %get-tuple-element.40), channel_id=1, source_target_pairs={{0,4},{4,8},{8,12},{12,16},{16,20},{20,24},{24,28},{28,32},{32,36}... | collective-permute-start | bytes 589832 | tf_op jit(solution)/shard_map/ppermute | solution.py:18
  13.0 1.2 copy-start.5
  13.1 7.7 %copy-start.1 = (f32[2,3,64,4,128]{2,4,3,1,0:T(8,128)S(1)}, f32[2,3,64,4,128]{2,4,3,1,0:T(8,128)}, u32[]{:S(2)}) copy-start(f32[2,3,64,4,128]{2,4,3,1,0:T(8,128)} %copy.146) | copy-start | bytes 2359300
  15.2 35.7 %collective-permute-start.1 = (f32[12,64,1,128]{3,1,2,0:T(8,128)}, f32[12,64,1,128]{3,1,2,0:T(8,128)}, u32[]{:S(2)}, u32[]{:S(2)}) collective-permute-start(f32[12,64,1,128]{3,1,2,0:T(8,128)} %get-tuple-element.31), channel_id=1, source_target_pairs={{4,0},{8,4},{12,8},{16,12},{20,16},{24,20},{28,24},{32,28},{36,32}... | collective-permute-start | bytes 1179656 | tf_op jit(solution)/shard_map/ppermute | solution.py:19
  18.3 32.6 %collective-permute-start = (f32[12,64,1,128]{3,1,2,0:T(8,128)}, f32[12,64,1,128]{3,1,2,0:T(8,128)}, u32[]{:S(2)}, u32[]{:S(2)}) collective-permute-start(f32[12,64,1,128]{3,1,2,0:T(8,128)} %get-tuple-element.30), channel_id=1, source_target_pairs={{0,4},{4,8},{8,12},{12,16},{16,20},{20,24},{24,28},{28,32},{32,36}... | collective-permute-start | bytes 1179656 | tf_op jit(solution)/shard_map/ppermute | solution.py:18
  36.5 5.0 copy-start.2
  42.2 6.3 %collective-permute-start.7 = (f32[6,64,6,1]{1,3,2,0:T(1,128)S(1)}, f32[6,64,6,1]{1,3,2,0:T(1,128)S(1)}, u32[]{:S(2)}, u32[]{:S(2)}) collective-permute-start(f32[6,64,6,1]{1,3,2,0:T(1,128)S(1)} %get-tuple-element.21), channel_id=1, source_target_pairs={{0,1},{1,2},{2,3},{4,5},{5,6},{6,7},{8,9},{9,10},{10,11},{12,13},{... | collective-permute-start | bytes 27656 | tf_op jit(solution)/shard_map/ppermute | solution.py:18
  44.8 4.5 collective-permute-start.6
  48.5 2.4 copy-start.6
  57.7 14.4 %collective-permute-start.3 = (f32[12,64,6,1]{1,3,2,0:T(1,128)S(1)}, f32[12,64,6,1]{1,3,2,0:T(1,128)S(1)}, u32[]{:S(2)}, u32[]{:S(2)}) collective-permute-start(f32[12,64,6,1]{1,3,2,0:T(1,128)S(1)} %copy.143), channel_id=1, source_target_pairs={{1,0},{2,1},{3,2},{5,4},{6,5},{7,6},{9,8},{10,9},{11,10},{13,12},{... | collective-permute-start | bytes 55304 | tf_op jit(solution)/shard_map/ppermute | solution.py:19
  61.5 12.9 %collective-permute-start.2 = (f32[12,64,6,1]{1,3,2,0:T(1,128)S(1)}, f32[12,64,6,1]{1,3,2,0:T(1,128)S(1)}, u32[]{:S(2)}, u32[]{:S(2)}) collective-permute-start(f32[12,64,6,1]{1,3,2,0:T(1,128)S(1)} %copy.142), channel_id=1, source_target_pairs={{0,1},{1,2},{2,3},{4,5},{5,6},{6,7},{8,9},{9,10},{10,11},{12,13},{... | collective-permute-start | bytes 55304 | tf_op jit(solution)/shard_map/ppermute | solution.py:18
  81.9 1.3 copy-start.7
  83.1 0.9 copy-start.14
  83.1 1.0 copy-start.15
  83.1 1.0 copy-start.16
  194.9 12.0 %copy-start.13 = (f32[64,4,128]{0,2,1:T(8,128)S(1)}, f32[64,4,128]{0,2,1:T(8,128)}, u32[]{:S(2)}) copy-start(f32[64,4,128]{0,2,1:T(8,128)} %get-tuple-element.22) | copy-start | bytes 393220
  198.6 12.4 %collective-permute-start.9 = (f32[12,64,1,128]{3,1,2,0:T(8,128)}, f32[12,64,1,128]{3,1,2,0:T(8,128)}, u32[]{:S(2)}, u32[]{:S(2)}) collective-permute-start(f32[12,64,1,128]{3,1,2,0:T(8,128)} %bitcast.36), channel_id=1, source_target_pairs={{4,0},{8,4},{12,8},{16,12},{20,16},{24,20},{28,24},{32,28},{36,32}... | collective-permute-start | bytes 1179656 | tf_op jit(solution)/shard_map/ppermute | solution.py:19
  201.1 12.0 %collective-permute-start.8 = (f32[12,64,1,128]{3,1,2,0:T(8,128)}, f32[12,64,1,128]{3,1,2,0:T(8,128)}, u32[]{:S(2)}, u32[]{:S(2)}) collective-permute-start(f32[12,64,1,128]{3,1,2,0:T(8,128)} %bitcast.35), channel_id=1, source_target_pairs={{0,4},{4,8},{8,12},{12,16},{16,20},{20,24},{24,28},{28,32},{32,36}... | collective-permute-start | bytes 1179656 | tf_op jit(solution)/shard_map/ppermute | solution.py:18
  215.3 6.6 %copy-start.9 = (f32[1,3,64,4,128]{2,4,3,1,0:T(8,128)S(1)}, f32[1,3,64,4,128]{2,4,3,1,0:T(8,128)}, u32[]{:S(2)}) copy-start(f32[1,3,64,4,128]{2,4,3,1,0:T(8,128)} %get-tuple-element.15) | copy-start | bytes 1179652
  215.3 6.6 %copy-start.10 = (f32[1,3,64,4,128]{2,4,3,1,0:T(8,128)S(1)}, f32[1,3,64,4,128]{2,4,3,1,0:T(8,128)}, u32[]{:S(2)}) copy-start(f32[1,3,64,4,128]{2,4,3,1,0:T(8,128)} %get-tuple-element.19) | copy-start | bytes 1179652
  215.3 6.6 %copy-start.11 = (f32[1,3,64,4,128]{2,4,3,1,0:T(8,128)S(1)}, f32[1,3,64,4,128]{2,4,3,1,0:T(8,128)}, u32[]{:S(2)}) copy-start(f32[1,3,64,4,128]{2,4,3,1,0:T(8,128)} %get-tuple-element.43) | copy-start | bytes 1179652
  216.6 9.8 %collective-permute-start.11 = (f32[12,64,6,1]{1,3,2,0:T(1,128)S(1)}, f32[12,64,6,1]{1,3,2,0:T(1,128)S(1)}, u32[]{:S(2)}, u32[]{:S(2)}) collective-permute-start(f32[12,64,6,1]{1,3,2,0:T(1,128)S(1)} %get-tuple-element.9), channel_id=1, source_target_pairs={{1,0},{2,1},{3,2},{5,4},{6,5},{7,6},{9,8},{10,9},{11,10},{13,12},{... | collective-permute-start | bytes 55304 | tf_op jit(solution)/shard_map/ppermute | solution.py:19
  217.9 8.5 %collective-permute-start.10 = (f32[12,64,6,1]{1,3,2,0:T(1,128)S(1)}, f32[12,64,6,1]{1,3,2,0:T(1,128)S(1)}, u32[]{:S(2)}, u32[]{:S(2)}) collective-permute-start(f32[12,64,6,1]{1,3,2,0:T(1,128)S(1)} %get-tuple-element.8), channel_id=1, source_target_pairs={{0,1},{1,2},{2,3},{4,5},{5,6},{6,7},{8,9},{9,10},{10,11},{12,13},{... | collective-permute-start | bytes 55304 | tf_op jit(solution)/shard_map/ppermute | solution.py:18
  239.4 4.2 copy-start.3
  239.4 4.5 copy-start.8
  243.9 0.9 copy-start.17
  243.9 1.0 copy-start.18
  342.9 1.1 copy-start.4
